TPU v7x, 32 devices: a whole 2x2x4 slice. The times are simulated.
32 devices in a mesh: grp: 2 (over x), tok: 4 (over z), head: 4 (over y, core).
Axes of the slice: x: 2, y: 2, z: 4, core: 2. Of those that a mesh axis runs over, the one named last changes fastest.
Arguments:
- views: bfloat16 [2, 2, 768, 1024], P('grp', None, 'tok'), may hold values from -6 to 6
- q_weight: bfloat16 [1024, 1024], P(None, 'head'), may hold values from -0.1875 to 0.1875
- k_weight: bfloat16 [1024, 1024], P(None, 'head'), may hold values from -0.1875 to 0.1875
- v_weight: bfloat16 [1024, 1024], P(None, 'head'), may hold values from -0.1875 to 0.1875
- rate_weight: bfloat16 [1024, 4], P(None, 'head'), may hold values from -0.1875 to 0.1875
- fast_in: float32 [4, 256, 1024], P('head', None, 'tok'), may hold values from -0.375 to 0.375
- fast_out: float32 [4, 512, 256], P('head', None, 'tok'), may hold values from -0.25 to 0.25
- out_gain: float32 [1024], P('head'), may hold values from 0.1 to 1.9
Outputs:
- rendered: bfloat16 [2, 2, 768, 1024], P('grp', None, 'tok', 'head')
All inputs are finite; a program needn't handle non-finite values.
Results may differ from a plain program's by a relative error of at most 0.013.
Values may be sent and summed in bfloat16 or wider, within the bound.
A program may use at most 64 MiB of HBM per device.

v0:
```python
import math

import jax
import jax.numpy as jnp
from jax import lax
from jax.sharding import PartitionSpec as P

norm_eps = 1e-06
out_eps = 1e-05
step_coef = 0.3
momentum_keep = 0.5


def spread(value, axis, source):
    kept = jnp.where(lax.axis_index(axis) == source, value, 0).astype(value.dtype)
    return lax.psum(kept, axis)


def rms_scale(values):
    return values * lax.rsqrt(jnp.mean(values * values, axis=-1, keepdims=True) + norm_eps)


def contract_rows(left, right):
    return lax.dot_general(
        left, right, (((0,), (0,)), ((), ())), preferred_element_type=jnp.float32
    )


def contract_cols(left, right):
    return lax.dot_general(
        left, right, (((1,), (1,)), ((), ())), preferred_element_type=jnp.float32
    )


def fast_apply(queries, copy_in, copy_out):
    hidden_units = copy_out.shape[0]
    pre_act = jnp.dot(queries, copy_in, preferred_element_type=jnp.float32)
    gate = pre_act[:, :hidden_units]
    upper = pre_act[:, hidden_units:]
    hidden = (gate * jax.nn.sigmoid(gate) * upper).astype(jnp.bfloat16)
    return jnp.dot(hidden, copy_out, preferred_element_type=jnp.float32)


def local(views, q_weight, k_weight, v_weight, rate_weight, fast_in, fast_out, out_gain):
    tok_count = lax.axis_size("tok")
    is_input = lax.axis_index("grp") == 0
    spans = views.shape[1]
    head_size = fast_in.shape[1]
    hidden_units = fast_out.shape[1]
    step_size = step_coef / math.sqrt(views.shape[2] * tok_count)
    width_all = head_size * lax.axis_size("head")
    whole_in, whole_out = (
        lax.all_gather(fast_in, "tok", axis=2, tiled=True),
        lax.all_gather(fast_out, "tok", axis=2, tiled=True),
    )
    whole_in = whole_in[0]
    whole_out = whole_out[0]
    copy_in = whole_in.astype(jnp.bfloat16)
    copy_out = whole_out.astype(jnp.bfloat16)
    state_in = fast_in[0]
    state_out = fast_out[0]
    base_in = jnp.mean(state_in * state_in, axis=0, keepdims=True)
    base_out = jnp.mean(state_out * state_out, axis=0, keepdims=True)
    moment_in = jnp.zeros_like(state_in)
    moment_out = jnp.zeros_like(state_out)

    def input_grads(inputs, given_in, given_out):
        keyed = rms_scale(jnp.dot(inputs, k_weight, preferred_element_type=jnp.float32)).astype(
            jnp.bfloat16
        )
        valued = jnp.dot(inputs, v_weight, preferred_element_type=jnp.float32)
        rates = jax.nn.softplus(jnp.dot(inputs, rate_weight, preferred_element_type=jnp.float32))
        upstream = (-(step_size * rates) * valued).astype(jnp.bfloat16)
        pre_act = jnp.dot(keyed, given_in, preferred_element_type=jnp.float32)
        gate = pre_act[:, :hidden_units]
        upper = pre_act[:, hidden_units:]
        sigma = jax.nn.sigmoid(gate)
        active = gate * sigma
        hidden = (active * upper).astype(jnp.bfloat16)
        grad_out = contract_rows(hidden, upstream)
        back = contract_cols(upstream, given_out)
        back_pre = jnp.concatenate(
            [back * upper * sigma * (1.0 + gate * (1.0 - sigma)), back * active], axis=1
        ).astype(jnp.bfloat16)
        grad_in = contract_rows(keyed, back_pre)
        return (grad_in, grad_out)

    def novel_grads(inputs, given_in, given_out):
        return (
            jnp.zeros((head_size, 2 * hidden_units), jnp.float32),
            jnp.zeros((hidden_units, head_size), jnp.float32),
        )

    outputs = []
    for span in range(spans):
        inputs = views[0, span]
        queries = rms_scale(jnp.dot(inputs, q_weight, preferred_element_type=jnp.float32)).astype(
            jnp.bfloat16
        )
        grads = lax.cond(is_input, input_grads, novel_grads, inputs, copy_in, copy_out)
        grad_in, grad_out = lax.psum_scatter(grads, "tok", scatter_dimension=1, tiled=True)
        moment_in = momentum_keep * moment_in + grad_in
        moment_out = momentum_keep * moment_out + grad_out
        trial_in = state_in - moment_in
        trial_out = state_out - moment_out
        mean_in = jnp.mean(trial_in * trial_in, axis=0, keepdims=True)
        mean_out = jnp.mean(trial_out * trial_out, axis=0, keepdims=True)
        state_in = trial_in * jnp.sqrt(base_in) * lax.rsqrt(mean_in + norm_eps)
        state_out = trial_out * jnp.sqrt(base_out) * lax.rsqrt(mean_out + norm_eps)
        part_in = state_in.astype(jnp.bfloat16)
        part_out = state_out.astype(jnp.bfloat16)
        copy_in, copy_out = (
            lax.all_gather(part_in, "tok", axis=1, tiled=True),
            lax.all_gather(part_out, "tok", axis=1, tiled=True),
        )
        copy_in, copy_out = (spread(copy_in, "grp", 0), spread(copy_out, "grp", 0))
        produced = fast_apply(queries, copy_in, copy_out)
        squares = lax.psum(jnp.sum(produced * produced, axis=1), "head")
        normed = produced * lax.rsqrt(squares / width_all + out_eps)[:, None] * out_gain
        outputs.append(normed.astype(jnp.bfloat16))
    return jnp.stack(outputs)[None]


def solution(mesh):
    placed = (
        P("grp", None, "tok", None),
        P(None, "head"),
        P(None, "head"),
        P(None, "head"),
        P(None, "head"),
        P("head", None, "tok"),
        P("head", None, "tok"),
        P("head"),
    )
    return jax.shard_map(
        local, mesh=mesh, in_specs=placed, out_specs=P("grp", None, "tok", "head"), check_vma=False
    )
```

profile of v0, /device:TPU:0, one launch (start us, length us, event | category | flops | bytes accessed | tf_op | source)
XLA Modules:
  0.0 281.3 jit_solution(5273160163596320403)
XLA Ops:
  6.5 1.2 slice_bitcast_fusion.1
  8.0 18.1 %all_gather.18 = bf16[1,512,256]{1,0,2:T(2,128)(2,1)} all-gather(bf16[1,512,64]{1,0,2:T(2,128)(2,1)S(1)} %copy.11), channel_id=1, replica_groups=mesh['grp'=2,'tok'=4,'head'=4] {'tok'}, dimensions={2}, use_global_device_ids=true | all-gather | bytes 327680 | tf_op jit(solution)/shard_map/all_gather | solution.py:54
  26.1 16.5 %all_gather.19 = bf16[1,256,1024]{2,1,0:T(8,128)(2,1)S(1)} all-gather(bf16[1,256,256]{2,1,0:T(8,128)(2,1)S(1)} %convert.16), channel_id=1, replica_groups=mesh['grp'=2,'tok'=4,'head'=4] {'tok'}, dimensions={2}, use_global_device_ids=true | all-gather | bytes 655360 | tf_op jit(solution)/shard_map/all_gather | solution.py:53
  42.6 7.0 %conditional.2 = (f32[256,1024]{1,0:T(8,128)S(1)}, f32[512,256]{1,0:T(8,128)}) conditional(s32[]{:T(128)} %convert_element_type.75, () %tuple.21, (bf16[192,1024]{1,0:T(8,128)(2,1)S(1)}, bf16[1024,256]{1,0:T(8,128)(2,1)S(1)}, bf16[1024,1]{0,1:T(2,128)(2,1)S(1)}, bf16[1024,256]{1,0:T(8,128)(2,1)S(1)}, bf16[1,512,256]{1,0,2:T(2,128)(2,1)}, ...), branch_computations={%region_1.0_spmd, %region_2.4_spmd} | conditional | flops 506758848 | bytes 14132096 | solution.py:100
  43.0 1.2 fusion.1
  44.8 0.7 copy-done.7
  46.0 1.4 multiply_convert_fusion.2
  48.6 1.1 fusion.12
  49.7 2.4 copy.18
  53.2 21.1 %reduce-scatter.13.cloned.1.call-done = f32[64,512]{1,0:T(8,128)} async-done(((f32[256,512]{1,0:T(8,128)}), f32[64,512]{1,0:T(8,128)}) %reduce-scatter.13.cloned.1.call-update) | async-done | bytes 131088
  74.3 1.0 copy.19
  75.6 15.5 %all_gather.21 = bf16[512,256]{0,1:T(8,128)(2,1)S(1)} all-gather(bf16[512,64]{0,1:T(8,128)(2,1)S(1)} %copy.14), channel_id=1, replica_groups=mesh['grp'=2,'tok'=4,'head'=4] {'tok'}, dimensions={1}, use_global_device_ids=true | all-gather | bytes 327680 | tf_op jit(solution)/shard_map/all_gather | solution.py:114
  91.9 11.3 %reduce-scatter.9.cloned.1.call-done = f32[256,256]{1,0:T(8,128)} async-done(((f32[256,1024]{1,0:T(8,128)}), f32[256,256]{1,0:T(8,128)}) %reduce-scatter.9.cloned.1.call-update) | async-done | bytes 262160 | tf_op jit(solution)/shard_map/reduce_scatter | solution.py:101
  103.2 1.1 fusion.34
  104.3 15.4 %all_gather.20 = bf16[256,1024]{1,0:T(8,128)(2,1)S(1)} all-gather(bf16[256,256]{1,0:T(8,128)(2,1)S(1)} %fusion.35), channel_id=1, replica_groups=mesh['grp'=2,'tok'=4,'head'=4] {'tok'}, dimensions={1}, use_global_device_ids=true | all-gather | bytes 655360 | tf_op jit(solution)/shard_map/all_gather | solution.py:113
  119.8 0.8 broadcast_select_fusion.1
  120.7 34.5 %all-reduce.8.cloned.1.call-done = (bf16[512,256]{0,1:T(8,128)(2,1)}, bf16[256,1024]{1,0:T(8,128)(2,1)}) async-done(((bf16[512,256]{0,1:T(8,128)(2,1)}, bf16[256,1024]{1,0:T(8,128)(2,1)}), (bf16[512,256]{0,1:T(8,128)(2,1)}, bf16[256,1024]{1,0:T(8,128)(2,1)})) %all-reduce.8.cloned.1.call-update) | async-done | bytes 786448 | tf_op jit(solution)/shard_map/psum | solution.py:16
  155.2 4.4 %conditional.3 = (f32[256,1024]{1,0:T(8,128)S(1)}, f32[512,256]{1,0:T(8,128)}) conditional(s32[]{:T(128)} %convert_element_type.75, () %tuple.23, (bf16[192,1024]{1,0:T(8,128)(2,1)S(1)}, bf16[1024,256]{1,0:T(8,128)(2,1)S(1)}, bf16[1024,1]{0,1:T(2,128)(2,1)S(1)}, bf16[1024,256]{1,0:T(8,128)(2,1)S(1)}, bf16[512,256]{0,1:T(8,128)(2,1)}, ...), branch_computations={%region_15.16_spmd, %region_16.18_spmd} | conditional | flops 506758848 | bytes 11772744 | solution.py:100
  158.4 1.1 fusion.24
  159.5 2.4 copy.20
  162.6 1.4 multiply_reduce_fusion.7
  164.4 19.5 %reduce-scatter.15.cloned.1.call-done = f32[64,512]{1,0:T(8,128)} async-done(((f32[256,512]{1,0:T(8,128)}), f32[64,512]{1,0:T(8,128)}) %reduce-scatter.15.cloned.1.call-update) | async-done | bytes 131088
  184.0 1.0 copy.21
  185.2 15.6 %all_gather.23 = bf16[512,256]{0,1:T(8,128)(2,1)S(1)} all-gather(bf16[512,64]{0,1:T(8,128)(2,1)S(1)} %copy.16), channel_id=1, replica_groups=mesh['grp'=2,'tok'=4,'head'=4] {'tok'}, dimensions={1}, use_global_device_ids=true | all-gather | bytes 327680 | tf_op jit(solution)/shard_map/all_gather | solution.py:114
  201.6 11.1 %reduce-scatter.11.cloned.1.call-done = f32[256,256]{1,0:T(8,128)} async-done(((f32[256,1024]{1,0:T(8,128)}), f32[256,256]{1,0:T(8,128)}) %reduce-scatter.11.cloned.1.call-update) | async-done | bytes 262160 | tf_op jit(solution)/shard_map/reduce_scatter | solution.py:101
  212.7 1.0 multiply_reduce_fusion.3
  213.8 15.8 %all_gather.22 = bf16[256,1024]{1,0:T(8,128)(2,1)S(1)} all-gather(bf16[256,256]{1,0:T(8,128)(2,1)S(1)} %multiply_convert_fusion.15), channel_id=1, replica_groups=mesh['grp'=2,'tok'=4,'head'=4] {'tok'}, dimensions={1}, use_global_device_ids=true | all-gather | bytes 655360 | tf_op jit(solution)/shard_map/all_gather | solution.py:113
  229.5 0.8 broadcast_select_fusion
  230.4 1.0 copy-done.8
  232.7 32.0 %all-reduce.6.cloned.1.call-done = (bf16[512,256]{0,1:T(8,128)(2,1)}, bf16[256,1024]{1,0:T(8,128)(2,1)}) async-done(((bf16[512,256]{0,1:T(8,128)(2,1)}, bf16[256,1024]{1,0:T(8,128)(2,1)}), (bf16[512,256]{0,1:T(8,128)(2,1)}, bf16[256,1024]{1,0:T(8,128)(2,1)})) %all-reduce.6.cloned.1.call-update) | async-done | bytes 786448 | tf_op jit(solution)/shard_map/psum | solution.py:16
  264.7 1.4 fusion.43
  266.5 6.4 %all-reduce = (f32[192]{0:T(256)S(1)}, f32[192]{0:T(256)S(1)}) all-reduce(f32[192]{0:T(256)S(1)} %get-tuple-element.95, f32[192]{0:T(256)S(1)} %get-tuple-element.97), channel_id=1, replica_groups=mesh['grp'=2,'tok'=4,'head'=4] {'head'}, use_global_device_ids=true, to_apply=%region_25.26 | all-reduce | flops 384 | bytes 3072 | tf_op jit(solution)/shard_map/psum | solution.py:118
  (94 shorter events, 13.2 us)
Async XLA Ops:
  6.5 156.1 %copy-start = (bf16[1024,256]{1,0:T(8,128)(2,1)S(1)}, bf16[1024,256]{1,0:T(8,128)(2,1)}, u32[]{:S(2)}) copy-start(bf16[1024,256]{1,0:T(8,128)(2,1)} %param.13) | copy-start | bytes 1572868
  6.5 67.8 %reduce-scatter.13.cloned.1.call-start = ((), (), s32[]{:S(2)}) async-start(), calls=%async_computation.6 | async-start | bytes 655360
  6.5 1.2 copy-start.12
  7.9 18.2 %copy-start.1 = (f32[1,256,256]{2,1,0:T(8,128)S(1)}, f32[1,256,256]{2,1,0:T(8,128)}, u32[]{:S(2)}) copy-start(f32[1,256,256]{2,1,0:T(8,128)} %param.17) | copy-start | bytes 786436
  7.9 34.7 %copy-start.16 = (bf16[1024,1]{0,1:T(2,128)(2,1)S(1)}, bf16[1024,1]{0,1:T(2,128)(2,1)}, u32[]{:S(2)}) copy-start(bf16[1024,1]{0,1:T(2,128)(2,1)} %param.16) | copy-start | bytes 6148
  26.1 16.5 %copy-start.5 = (bf16[1024,256]{1,0:T(8,128)(2,1)S(1)}, bf16[1024,256]{1,0:T(8,128)(2,1)}, u32[]{:S(2)}) copy-start(bf16[1024,256]{1,0:T(8,128)(2,1)} %param.14) | copy-start | bytes 1572868
  26.1 16.5 %copy-start.6 = (bf16[1024,256]{1,0:T(8,128)(2,1)S(1)}, bf16[1024,256]{1,0:T(8,128)(2,1)}, u32[]{:S(2)}) copy-start(bf16[1024,256]{1,0:T(8,128)(2,1)} %param.15) | copy-start | bytes 1572868
  44.4 1.1 copy-start.7
  44.8 1.2 copy-start.14
  47.4 1.1 copy-start.11
  47.4 1.1 copy-start.15
  49.7 2.5 copy-start.2
  52.1 51.1 %reduce-scatter.9.cloned.1.call-start = ((), (), s32[]{:S(2)}) async-start(), calls=%async_computation.4 | async-start | bytes 1310720 | tf_op jit(solution)/shard_map/reduce_scatter | solution.py:101
  52.2 0.9 copy-start.13
  52.9 102.3 %all-reduce.8.cloned.1.call-start = ((), (), s32[]{:S(2)}) async-start(), calls=%async_computation.9 | async-start | bytes 1572864 | tf_op jit(solution)/shard_map/psum | solution.py:16
  103.2 1.1 copy-start.4
  120.6 63.3 %reduce-scatter.15.cloned.1.call-start = ((), (), s32[]{:S(2)}) async-start(), calls=%async_computation.7 | async-start | bytes 655360
  155.2 1.0 copy-start.9
  156.8 1.0 copy-start.19
  159.5 2.5 copy-start.3
  162.0 50.7 %reduce-scatter.11.cloned.1.call-start = ((), (), s32[]{:S(2)}) async-start(), calls=%async_computation.5 | async-start | bytes 1310720 | tf_op jit(solution)/shard_map/reduce_scatter | solution.py:101
  162.5 1.5 copy-start.10
  162.6 102.2 %all-reduce.6.cloned.1.call-start = ((), (), s32[]{:S(2)}) async-start(), calls=%async_computation.8 | async-start | bytes 1572864 | tf_op jit(solution)/shard_map/psum | solution.py:16
  230.4 1.0 copy-start.8
  231.4 0.9 copy-start.18
  264.7 1.4 copy-start.20
  272.9 0.7 copy-start.17
Sparse Core Ops, SparseCore 0:
  52.2 22.0 reduce-scatter.12
  76.6 26.4 reduce-scatter.8
  120.7 34.3 all-reduce.7
  162.1 21.8 reduce-scatter.14
  186.1 26.5 reduce-scatter.10
  230.5 34.1 all-reduce.5
where the time goes:
time: 282 us; the launch traced here: 281 us
  waiting for transfers between devices  131 us (46%)
  blocking collectives  103 us (37%)
  local copies, waits for them, and re-layouts  14.3 us (5%)
  between operations  13.7 us (5%)
  matrix products  12.1 us (4%)
  other arithmetic  6.49 us (2%)
    psum x2, waiting for transfers between devices, spread(): return lax.psum(kept, axis)  66.5 us
    unnamed x8, waiting for transfers between devices  41.9 us
    all_gather x2, blocking collectives, local(): lax.all_gather(part_in, 'tok', axis=1, tiled=True)  31.2 us
    all_gather x2, blocking collectives, local(): lax.all_gather(part_out, 'tok', axis=1, tiled=True)  31.2 us
    reduce_scatter x2, waiting for transfers between devices, local(): lax.psum_scatter(grads, 'tok', scatter_dimension=1, tiled=True)  22.4 us
    all_gather x1, blocking collectives, local(): lax.all_gather(fast_out, 'tok', axis=2, tiled=True)  18.1 us
    all_gather x1, blocking collectives, local(): lax.all_gather(fast_in, 'tok', axis=2, tiled=True)  16.5 us
    unnamed x36, local copies, waits for them, and re-layouts  9.64 us
  transfers between devices with their start and end apart: 6, of which 6 were waited for; matrix products, arithmetic and copies ran while one was open for 2% of the time, Pallas kernels for 0%

commit v1 on v0

--- a/solution.py
+++ b/solution.py
@@ -1,8 +1,11 @@
+import functools
 import math
 
 import jax
 import jax.numpy as jnp
 from jax import lax
+from jax.experimental import pallas as pl
+from jax.experimental.pallas import tpu as pltpu
 from jax.sharding import PartitionSpec as P
 
 norm_eps = 1e-06
@@ -41,7 +44,7 @@
     return jnp.dot(hidden, copy_out, preferred_element_type=jnp.float32)
 
 
-def local(views, q_weight, k_weight, v_weight, rate_weight, fast_in, fast_out, out_gain):
+def by_collectives(views, q_weight, k_weight, v_weight, rate_weight, fast_in, fast_out, out_gain):
     tok_count = lax.axis_size("tok")
     is_input = lax.axis_index("grp") == 0
     spans = views.shape[1]
@@ -121,7 +124,335 @@
     return jnp.stack(outputs)[None]
 
 
+def fused_kernel(
+    tok_count, grp_count, head_count,
+    views_ref, q_ref, k_ref, v_ref, rate_ref, in_ref, out_ref, gain_ref,
+    res_ref,
+    pieces, packed, queries, moment_in, moment_out, state_in, state_out, copy_in, copy_out,
+    base_in, base_out, produced, squares,
+    local_sem,
+    first_send, first_recv, z_send, z_recv, x_send, x_recv, y_send, y_recv,
+    c1_send, c1_recv, c2_send, c2_recv, wz_send, wz_recv, wx_send, wx_recv, sq_send, sq_recv,
+):
+    tok, grp, head = lax.axis_index("tok"), lax.axis_index("grp"), lax.axis_index("head")
+    spans, rows, width = views_ref.shape[1:]
+    piece = pieces.shape[-1]
+    head_size, block_in = in_ref.shape[1:]
+    hidden_units, block_out = out_ref.shape[1:]
+    pack = packed.shape[-1] - block_in
+    folds = pack // block_out
+    half = head_size // grp_count
+    step_size = step_coef / math.sqrt(rows * tok_count)
+    other_grp = {"grp": 1 - grp}
+    far_bit = head_count // 2
+    far_head = jnp.where(head < far_bit, head + far_bit, head - far_bit)
+    flip = 1 - 2 * lax.rem(head, 2)
+    near_head = head + flip
+    far = {"head": far_head}
+    near = {"head": near_head}
+
+    def shard(step):
+        return lax.rem(tok - step + tok_count, tok_count)
+
+    def peer(step):
+        return {"tok": lax.rem(tok + step, tok_count)}
+
+    def remote(src, dst, send, recv, target):
+        return pltpu.make_async_remote_copy(
+            src_ref=src, dst_ref=dst, send_sem=send, recv_sem=recv,
+            device_id=target, device_id_type=pl.DeviceIdType.MESH,
+        )
+
+    def view_piece(span, part):
+        start = pl.multiple_of((head * grp_count + part) * piece, piece)
+        return views_ref.at[0, span, :, pl.ds(start, piece)]
+
+    def same(ref, send, recv, target):
+        return remote(ref, ref, send, recv, target)
+
+    own = [
+        pltpu.make_async_copy(view_piece(s, 0), pieces.at[s, tok, head, 0], local_sem.at[s])
+        for s in range(spans)
+    ]
+    first = [
+        remote(view_piece(s, 1), pieces.at[s, tok, head, 1], first_send.at[s], first_recv.at[s], other_grp)
+        for s in range(spans)
+    ]
+    along_z = [
+        [
+            same(pieces.at[s, tok, head, grp], z_send.at[s, d], z_recv.at[s, d], peer(d + 1))
+            for d in range(tok_count - 1)
+        ]
+        for s in range(spans)
+    ]
+    along_x = [
+        [
+            same(pieces.at[s, shard(d), head, grp], x_send.at[s, d], x_recv.at[s, d], other_grp)
+            for d in range(tok_count)
+        ]
+        for s in range(spans)
+    ]
+    along_y = [
+        [
+            same(pieces.at[s, shard(d), head], y_send.at[s, d], y_recv.at[s, d], far)
+            for d in range(tok_count)
+        ]
+        for s in range(spans)
+    ]
+    core_own = [
+        [
+            same(pieces.at[s, shard(d), head], c1_send.at[s, d], c1_recv.at[s, d], near)
+            for d in range(tok_count)
+        ]
+        for s in range(spans)
+    ]
+    core_far = [
+        [
+            same(pieces.at[s, shard(d), far_head], c2_send.at[s, d], c2_recv.at[s, d], near)
+            for d in range(tok_count)
+        ]
+        for s in range(spans)
+    ]
+    my_half = pl.ds(pl.multiple_of(grp * half, half), half)
+    fast_z = [
+        same(packed.at[tok, my_half], wz_send.at[d], wz_recv.at[d], peer(d + 1))
+        for d in range(tok_count - 1)
+    ]
+    fast_x = [
+        same(packed.at[shard(d + 1), my_half], wx_send.at[d], wx_recv.at[d], other_grp)
+        for d in range(tok_count - 1)
+    ]
+    square = [
+        [
+            same(squares.at[s, head], sq_send.at[s, d], sq_recv.at[s, d],
+                 {"head": lax.rem(head + d + 1, head_count)})
+            for d in range(head_count - 1)
+        ]
+        for s in range(spans)
+    ]
+
+    barrier = pltpu.get_barrier_semaphore()
+    partners = [peer(d + 1) for d in range(tok_count - 1)] + [other_grp]
+    partners += [{"head": lax.rem(head + d + 1, head_count)} for d in range(head_count - 1)]
+    for target in partners:
+        pl.semaphore_signal(barrier, inc=1, device_id=target, device_id_type=pl.DeviceIdType.MESH)
+
+    @pl.when(grp == 0)
+    def _():
+        for copy in own:
+            copy.start()
+
+    packed[tok, :, :block_in] = in_ref[0].astype(jnp.bfloat16)
+    fold_rows = hidden_units // folds
+    packed[tok, :, block_in:] = jnp.concatenate(
+        [out_ref[0, f * fold_rows:(f + 1) * fold_rows, :] for f in range(folds)], axis=1
+    ).astype(jnp.bfloat16)
+    pl.semaphore_wait(barrier, len(partners))
+
+    @pl.when(grp == 0)
+    def _():
+        for s in range(spans):
+            first[s].start()
+        for copy in own:
+            copy.wait()
+        for copy in along_z[0]:
+            copy.start()
+
+    for copy in fast_z:
+        copy.start()
+
+    @pl.when(grp == 1)
+    def _():
+        first[0].wait_recv()
+        for copy in along_z[0]:
+            copy.start()
+
+    along_x[0][0].start()
+
+    @pl.when(grp == 1)
+    def _():
+        first[1].wait_recv()
+
+    for s in range(1, spans):
+        for copy in along_z[s]:
+            copy.start()
+    for s in range(spans):
+        queries[s] = rms_scale(
+            jnp.dot(views_ref[0, s], q_ref[...], preferred_element_type=jnp.float32)
+        ).astype(jnp.bfloat16)
+    for d in range(tok_count - 1):
+        along_z[0][d].wait_recv()
+        along_x[0][d + 1].start()
+    for d in range(tok_count - 1):
+        fast_z[d].wait_recv()
+        fast_x[d].start()
+    along_x[1][0].start()
+    for d in range(tok_count):
+        along_x[0][d].wait_recv()
+        along_y[0][d].start()
+        core_own[0][d].start()
+    for d in range(tok_count - 1):
+        along_z[1][d].wait_recv()
+        along_x[1][d + 1].start()
+    for d in range(tok_count):
+        along_y[0][d].wait_recv()
+        core_far[0][d].start()
+    for d in range(tok_count):
+        along_x[1][d].wait_recv()
+        along_y[1][d].start()
+        core_own[1][d].start()
+    for d in range(tok_count - 1):
+        fast_x[d].wait_recv()
+
+    for t in range(tok_count):
+        cols = slice(t * block_in, (t + 1) * block_in)
+        given = packed[t, :, :block_in]
+        wide = given.astype(jnp.float32)
+        copy_in[:, cols] = given
+        state_in[:, cols] = wide
+        base_in[:, cols] = jnp.sqrt(jnp.mean(wide * wide, axis=0, keepdims=True))
+    for f in range(folds):
+        given = jnp.concatenate(
+            [packed[t, :, block_in + f * block_out:block_in + (f + 1) * block_out].astype(jnp.float32)
+             for t in range(tok_count)], axis=1
+        )
+        copy_out[f * fold_rows:(f + 1) * fold_rows, :] = given.astype(jnp.bfloat16)
+        state_out[f * fold_rows:(f + 1) * fold_rows, :] = given
+    base_out[...] = jnp.sqrt(jnp.mean(state_out[...] * state_out[...], axis=0, keepdims=True))
+    moment_in[...] = jnp.zeros_like(moment_in)
+    moment_out[...] = jnp.zeros_like(moment_out)
+
+    def add_grads(span, t):
+        inputs = jnp.concatenate(
+            [pieces[span, t, h, g] for h in range(head_count) for g in range(grp_count)], axis=1
+        )
+        keyed = rms_scale(jnp.dot(inputs, k_ref[...], preferred_element_type=jnp.float32)).astype(
+            jnp.bfloat16
+        )
+        valued = jnp.dot(inputs, v_ref[...], preferred_element_type=jnp.float32)
+        raw = jnp.dot(inputs, rate_ref[...], preferred_element_type=jnp.float32)[:, :1]
+        rates = jnp.maximum(raw, 0.0) + jnp.log1p(jnp.exp(-jnp.abs(raw)))
+        upstream = (-(step_size * rates) * valued).astype(jnp.bfloat16)
+        gate = jnp.dot(keyed, copy_in[:, :hidden_units], preferred_element_type=jnp.float32)
+        upper = jnp.dot(keyed, copy_in[:, hidden_units:], preferred_element_type=jnp.float32)
+        sigma = jax.nn.sigmoid(gate)
+        active = gate * sigma
+        hidden = (active * upper).astype(jnp.bfloat16)
+        moment_out[...] += contract_rows(hidden, upstream)
+        back = contract_cols(upstream, copy_out[...])
+        back_gate = (back * upper * sigma * (1.0 + gate * (1.0 - sigma))).astype(jnp.bfloat16)
+        back_upper = (back * active).astype(jnp.bfloat16)
+        moment_in[:, :hidden_units] += contract_rows(keyed, back_gate)
+        moment_in[:, hidden_units:] += contract_rows(keyed, back_upper)
+
+    def renormalize(state, moment, base, copy, cols):
+        trial = state[:, cols] - moment[:, cols]
+        mean = jnp.mean(trial * trial, axis=0, keepdims=True)
+        state[:, cols] = trial * base[:, cols] * lax.rsqrt(mean + norm_eps)
+        copy[:, cols] = state[:, cols].astype(jnp.bfloat16)
+        moment[:, cols] = moment[:, cols] * momentum_keep
+
+    for s in range(spans):
+        for d in range(tok_count):
+            core_own[s][d].wait_recv()
+            core_far[s][d].wait_recv()
+        lax.fori_loop(0, tok_count, lambda t, c: (add_grads(s, t), c)[1], 0)
+        if s + 1 < spans:
+            for d in range(tok_count):
+                along_y[s + 1][d].wait_recv()
+                core_far[s + 1][d].start()
+        for t in range(tok_count):
+            renormalize(state_in, moment_in, base_in, copy_in, slice(t * block_in, (t + 1) * block_in))
+        renormalize(state_out, moment_out, base_out, copy_out, slice(None))
+        made = fast_apply(queries[s], copy_in[...], copy_out[...])
+        produced[s] = made
+        sums = jnp.sum(made * made, axis=1, keepdims=True)
+        squares[s, head] = jnp.transpose(jnp.broadcast_to(sums, (rows, 128)))[:8]
+        for copy in square[s]:
+            copy.start()
+
+    for s in range(spans):
+        for copy in square[s]:
+            copy.wait_recv()
+        total = squares[s, 0]
+        for h in range(1, head_count):
+            total = total + squares[s, h]
+        scale = lax.rsqrt(total / (head_size * head_count) + out_eps)
+        column = jnp.transpose(jnp.concatenate([scale] * 16, axis=0))[:, :1]
+        res_ref[0, s] = (produced[s] * column * gain_ref[...]).astype(jnp.bfloat16)
+
+    @pl.when(grp == 0)
+    def _():
+        for copy in first:
+            copy.wait_send()
+
+    for group in (along_z, along_x, along_y, core_own, core_far, square):
+        for copies in group:
+            for copy in copies:
+                copy.wait_send()
+    for copy in fast_z + fast_x:
+        copy.wait_send()
+
+
+def by_kernel(sizes, views, q_weight, k_weight, v_weight, rate_weight, fast_in, fast_out, out_gain):
+    tok_count, grp_count, head_count = sizes
+    _, spans, rows, width = views.shape
+    _, head_size, block_in = fast_in.shape
+    _, hidden_units, block_out = fast_out.shape
+    piece = width // (grp_count * head_count)
+    pack = block_out * (hidden_units // head_size)
+    dma = pltpu.SemaphoreType.DMA
+    vmem = pltpu.VMEM
+    pair = [dma((spans, tok_count))] * 2
+    return pl.pallas_call(
+        functools.partial(fused_kernel, tok_count, grp_count, head_count),
+        out_shape=jax.ShapeDtypeStruct((1, spans, rows, head_size), jnp.bfloat16),
+        in_specs=[pl.BlockSpec(memory_space=pltpu.VMEM)] * 8,
+        out_specs=pl.BlockSpec(memory_space=pltpu.VMEM),
+        scratch_shapes=[
+            vmem((spans, tok_count, head_count, grp_count, rows, piece), jnp.bfloat16),
+            vmem((tok_count, head_size, block_in + pack), jnp.bfloat16),
+            vmem((spans, rows, head_size), jnp.bfloat16),
+            vmem((head_size, 2 * hidden_units), jnp.float32),
+            vmem((hidden_units, head_size), jnp.float32),
+            vmem((head_size, 2 * hidden_units), jnp.float32),
+            vmem((hidden_units, head_size), jnp.float32),
+            vmem((head_size, 2 * hidden_units), jnp.bfloat16),
+            vmem((hidden_units, head_size), jnp.bfloat16),
+            vmem((1, 2 * hidden_units), jnp.float32),
+            vmem((1, head_size), jnp.float32),
+            vmem((spans, rows, head_size), jnp.float32),
+            vmem((spans, head_count, 8, rows), jnp.float32),
+            dma((spans,)),
+            *[dma((spans,))] * 2,
+            *[dma((spans, tok_count - 1))] * 2,
+            *pair, *pair, *pair, *pair,
+            *[dma((tok_count - 1,))] * 4,
+            *[dma((spans, head_count - 1))] * 2,
+        ],
+        compiler_params=pltpu.CompilerParams(collective_id=0, has_side_effects=True),
+        name="fused_layer",
+    )(views, q_weight, k_weight, v_weight, rate_weight, fast_in, fast_out, out_gain.reshape(1, -1))
+
+
+def local(sizes, views, *rest):
+    tok_count, grp_count, head_count = sizes
+    fast_in, fast_out = rest[4], rest[5]
+    head_size, hidden_units = fast_in.shape[1], fast_out.shape[1]
+    piece = views.shape[3] // (grp_count * head_count)
+    few = tok_count * views.shape[2] <= 4 * head_size
+    fits = (
+        tok_count > 1 and grp_count == 2 and head_count == 4 and piece % 128 == 0
+        and fast_in.shape[2] % 128 == 0 and views.shape[2] % 16 == 0 and hidden_units % head_size == 0
+        and fast_out.shape[2] * (hidden_units // head_size) % 128 == 0
+    )
+    if few and fits:
+        return by_kernel(sizes, views, *rest)
+    return by_collectives(views, *rest)
+
+
 def solution(mesh):
+    sizes = (mesh.shape["tok"], mesh.shape["grp"], mesh.shape["head"])
     placed = (
         P("grp", None, "tok", None),
         P(None, "head"),
@@ -133,5 +464,5 @@
         P("head"),
     )
     return jax.shard_map(
-        local, mesh=mesh, in_specs=placed, out_specs=P("grp", None, "tok", "head"), check_vma=False
-    )
+        functools.partial(local, sizes), mesh=mesh, in_specs=placed, out_specs=P("grp", None, "tok", "head"), check_vma=False
+    )

time: 282 us -> 56.8 us (0.20)
  waiting for transfers between devices: 131 us -> 0 us
  blocking collectives: 103 us -> 0 us
  Pallas kernels: 0 us -> 52.5 us
  between operations: 13.7 us -> 0.01 us
  matrix products: 12.1 us -> 0 us
  local copies, waits for them, and re-layouts: 14.3 us -> 4.04 us
  other arithmetic: 6.49 us -> 0 us
    all_gather x6 -> x0, blocking collectives: 97 us -> none  [the longest x2 31.2 us: local(): lax.all_gather(part_in, 'tok', axis=1, tiled=True)]
    psum x2 -> x0, waiting for transfers between devices: 66.5 us -> none  [spread(): return lax.psum(kept, axis)]
    pallas_call x0 -> x1, Pallas kernels: none -> 52.5 us  [by_kernel(): pl.pallas_call(functools.partial(fused_kernel, tok_count, grp_count, head...]
    unnamed x8 -> x0, waiting for transfers between devices: 41.9 us -> none
    reduce_scatter x2 -> x0, waiting for transfers between devices: 22.4 us -> none  [local(): lax.psum_scatter(grads, 'tok', scatter_dimension=1, tiled=True)]
    dot_general x20 -> x0, matrix products: 12.1 us -> none  [the longest x4 3.04 us: contract_rows(): lax.dot_general(left, right, (((0,), (0,)), ((), ())), preferred_element_...]
    psum x1 -> x0, blocking collectives: 6.4 us -> none  [local(): squares = lax.psum(jnp.sum(produced * produced, axis=1), 'head')]
    unnamed x36 -> x5, local copies, waits for them, and re-layouts: 9.64 us -> 4.04 us
  transfers between devices with their start and end apart: 6 -> 0, of which waited for: 6 -> 0; matrix products, arithmetic and copies ran while one was open for 2% -> 0% of each run, Pallas kernels for 0% -> 0%
where the time goes in v1:
time: 56.8 us; the launch traced here: 56.6 us
  Pallas kernels  52.5 us (92%)
  local copies, waits for them, and re-layouts  4.04 us (7%)
    pallas_call x1, Pallas kernels, by_kernel(): pl.pallas_call(functools.partial(fused_kernel, tok_count, grp_count, head...  52.5 us
    unnamed x5, local copies, waits for them, and re-layouts  4.04 us

profile of v1, /device:TPU:0, one launch (start us, length us, event | category | flops | bytes accessed | tf_op | source)
XLA Modules:
  0.0 56.6 jit_solution(11466790447496611750)
XLA Ops:
  0.0 0.0 copy-start
  0.0 1.6 %copy.9.rate_ref = bf16[1024,1]{1,0:T(8,128)(2,1)} copy(bf16[1024,1]{0,1:T(2,128)(2,1)} %param.12) | data formatting | bytes 4096 | tf_op args[4]
  1.6 0.0 copy-done
  1.6 0.8 %copy.10.out_ref = f32[1,512,64]{2,1,0:T(8,128)} copy(f32[1,512,64]{1,2,0:T(8,128)S(1)} %copy-done) | data formatting | bytes 262144 | tf_op args[6]
  2.4 52.5 %fused_layer.1 = bf16[1,2,192,256]{3,2,1,0:T(8,128)(2,1)} custom-call(bf16[1,2,192,1024]{3,2,1,0:T(8,128)(2,1)} %views_ref.1, bf16[1024,256]{1,0:T(8,128)(2,1)} %q_ref.1, bf16[1024,256]{1,0:T(8,128)(2,1)} %k_ref.1, bf16[1024,256]{1,0:T(8,128)(2,1)} %v_ref.1, bf16[1024,1]{1,0:T(8,128)(2,1)} %copy.9.rate_ref, f32[1,256,256]{2,1,0:T(8,128)} %in_ref.1, ...), custom_call_target="tpu_custom_call" | custom-call | tf_op jit(solution)/shard_map/fused_layer/pallas_call | solution.py:407
  55.0 1.6 %copy.12 = bf16[1,2,192,256]{3,2,1,0:T(8,128)(2,1)} copy(bf16[1,2,192,256]{3,2,1,0:T(8,128)(2,1)} %fused_layer.1) | data formatting | bytes 393216
Async XLA Ops:
  0.0 1.6 %copy-start = (f32[1,512,64]{1,2,0:T(8,128)S(1)}, f32[1,512,64]{1,2,0:T(8,128)}, u32[]{:S(2)}) copy-start(f32[1,512,64]{1,2,0:T(8,128)} %param.14) | copy-start | bytes 393220

commit v2 on v1

--- a/solution.py
+++ b/solution.py
@@ -128,7 +128,7 @@
     tok_count, grp_count, head_count,
     views_ref, q_ref, k_ref, v_ref, rate_ref, in_ref, out_ref, gain_ref,
     res_ref,
-    pieces, packed, queries, moment_in, moment_out, state_in, state_out, copy_in, copy_out,
+    pieces, packed, queries, keys, ups, moment_in, moment_out, state_in, state_out, copy_in, copy_out,
     base_in, base_out, produced, squares,
     local_sem,
     first_send, first_recv, z_send, z_recv, x_send, x_recv, y_send, y_recv,
@@ -138,9 +138,9 @@
     spans, rows, width = views_ref.shape[1:]
     piece = pieces.shape[-1]
     head_size, block_in = in_ref.shape[1:]
-    hidden_units, block_out = out_ref.shape[1:]
-    pack = packed.shape[-1] - block_in
-    folds = pack // block_out
+    block_out, hidden_units = out_ref.shape[1:]
+    fold = packed.shape[-1] - block_in
+    folds = hidden_units // fold
     half = head_size // grp_count
     step_size = step_coef / math.sqrt(rows * tok_count)
     other_grp = {"grp": 1 - grp}
@@ -243,10 +243,10 @@
             copy.start()
 
     packed[tok, :, :block_in] = in_ref[0].astype(jnp.bfloat16)
-    fold_rows = hidden_units // folds
-    packed[tok, :, block_in:] = jnp.concatenate(
-        [out_ref[0, f * fold_rows:(f + 1) * fold_rows, :] for f in range(folds)], axis=1
-    ).astype(jnp.bfloat16)
+    for f in range(folds):
+        packed[tok, f * block_out:(f + 1) * block_out, block_in:] = out_ref[
+            0, :, f * fold:(f + 1) * fold
+        ].astype(jnp.bfloat16)
     pl.semaphore_wait(barrier, len(partners))
 
     @pl.when(grp == 0)
@@ -258,9 +258,6 @@
         for copy in along_z[0]:
             copy.start()
 
-    for copy in fast_z:
-        copy.start()
-
     @pl.when(grp == 1)
     def _():
         first[0].wait_recv()
@@ -271,36 +268,71 @@
 
     @pl.when(grp == 1)
     def _():
-        first[1].wait_recv()
+        for s in range(1, spans):
+            first[s].wait_recv()
 
     for s in range(1, spans):
+        along_x[s][0].start()
         for copy in along_z[s]:
             copy.start()
+    for copy in fast_z:
+        copy.start()
+
+    def project_queries(span):
+        queries[span] = rms_scale(
+            jnp.dot(views_ref[0, span], q_ref[...], preferred_element_type=jnp.float32)
+        ).astype(jnp.bfloat16)
+
+    def project(span, t):
+        inputs = jnp.concatenate(
+            [pieces[span, t, h, g] for h in range(head_count) for g in range(grp_count)], axis=1
+        )
+        keys[span, t] = rms_scale(
+            jnp.dot(inputs, k_ref[...], preferred_element_type=jnp.float32)
+        ).astype(jnp.bfloat16)
+        valued = jnp.dot(inputs, v_ref[...], preferred_element_type=jnp.float32)
+        raw = contract_cols(inputs, jnp.broadcast_to(rate_ref[...], (8, width)))[:, :1]
+        rates = jnp.maximum(raw, 0.0) + jnp.log1p(jnp.exp(-jnp.abs(raw)))
+        ups[span, t] = (-(step_size * rates) * valued).astype(jnp.bfloat16)
+
+    def forward(span, step):
+        if 1 <= step - 1 < tok_count:
+            along_x[span][step - 1].wait_recv()
+            along_y[span][step - 1].start()
+            core_own[span][step - 1].start()
+        if 0 <= step - 2 < tok_count:
+            along_y[span][step - 2].wait_recv()
+            core_far[span][step - 2].start()
+        if 0 <= step - 3 < tok_count:
+            core_own[span][step - 3].wait_recv()
+            core_far[span][step - 3].wait_recv()
+            project(span, shard(step - 3))
+
+    def pass_on(span, step):
+        along_z[span][step - 1].wait_recv()
+        along_x[span][step].start()
+
+    last_step = tok_count + 2
     for s in range(spans):
-        queries[s] = rms_scale(
-            jnp.dot(views_ref[0, s], q_ref[...], preferred_element_type=jnp.float32)
-        ).astype(jnp.bfloat16)
-    for d in range(tok_count - 1):
-        along_z[0][d].wait_recv()
-        along_x[0][d + 1].start()
+        along_x[s][0].wait_recv()
+        along_y[s][0].start()
+        core_own[s][0].start()
+    project_queries(0)
+    for step in range(1, last_step + 1):
+        if step < tok_count:
+            pass_on(0, step)
+        forward(0, step)
+        for s in range(1, spans):
+            if 0 <= step - tok_count < tok_count - 1:
+                pass_on(s, step - tok_count + 1)
     for d in range(tok_count - 1):
         fast_z[d].wait_recv()
         fast_x[d].start()
-    along_x[1][0].start()
-    for d in range(tok_count):
-        along_x[0][d].wait_recv()
-        along_y[0][d].start()
-        core_own[0][d].start()
-    for d in range(tok_count - 1):
-        along_z[1][d].wait_recv()
-        along_x[1][d + 1].start()
-    for d in range(tok_count):
-        along_y[0][d].wait_recv()
-        core_far[0][d].start()
-    for d in range(tok_count):
-        along_x[1][d].wait_recv()
-        along_y[1][d].start()
-        core_own[1][d].start()
+    for s in range(1, spans):
+        for step in range(1, tok_count + 1):
+            forward(s, step)
+    for s in range(1, spans):
+        project_queries(s)
     for d in range(tok_count - 1):
         fast_x[d].wait_recv()
 
@@ -311,60 +343,58 @@
         copy_in[:, cols] = given
         state_in[:, cols] = wide
         base_in[:, cols] = jnp.sqrt(jnp.mean(wide * wide, axis=0, keepdims=True))
-    for f in range(folds):
-        given = jnp.concatenate(
-            [packed[t, :, block_in + f * block_out:block_in + (f + 1) * block_out].astype(jnp.float32)
-             for t in range(tok_count)], axis=1
-        )
-        copy_out[f * fold_rows:(f + 1) * fold_rows, :] = given.astype(jnp.bfloat16)
-        state_out[f * fold_rows:(f + 1) * fold_rows, :] = given
-    base_out[...] = jnp.sqrt(jnp.mean(state_out[...] * state_out[...], axis=0, keepdims=True))
+        for f in range(folds):
+            part = slice(f * fold, (f + 1) * fold)
+            turned = slice(t * block_out, (t + 1) * block_out)
+            given = packed[t, f * block_out:(f + 1) * block_out, block_in:]
+            copy_out[turned, part] = given
+            state_out[turned, part] = given.astype(jnp.float32)
+    base_out[...] = jnp.sqrt(jnp.mean(state_out[...] * state_out[...], axis=1, keepdims=True))
     moment_in[...] = jnp.zeros_like(moment_in)
     moment_out[...] = jnp.zeros_like(moment_out)
 
     def add_grads(span, t):
-        inputs = jnp.concatenate(
-            [pieces[span, t, h, g] for h in range(head_count) for g in range(grp_count)], axis=1
-        )
-        keyed = rms_scale(jnp.dot(inputs, k_ref[...], preferred_element_type=jnp.float32)).astype(
-            jnp.bfloat16
-        )
-        valued = jnp.dot(inputs, v_ref[...], preferred_element_type=jnp.float32)
-        raw = jnp.dot(inputs, rate_ref[...], preferred_element_type=jnp.float32)[:, :1]
-        rates = jnp.maximum(raw, 0.0) + jnp.log1p(jnp.exp(-jnp.abs(raw)))
-        upstream = (-(step_size * rates) * valued).astype(jnp.bfloat16)
+        keyed, upstream = keys[span, t], ups[span, t]
         gate = jnp.dot(keyed, copy_in[:, :hidden_units], preferred_element_type=jnp.float32)
         upper = jnp.dot(keyed, copy_in[:, hidden_units:], preferred_element_type=jnp.float32)
         sigma = jax.nn.sigmoid(gate)
         active = gate * sigma
         hidden = (active * upper).astype(jnp.bfloat16)
-        moment_out[...] += contract_rows(hidden, upstream)
-        back = contract_cols(upstream, copy_out[...])
+        moment_out[...] += contract_rows(upstream, hidden)
+        back = jnp.dot(upstream, copy_out[...], preferred_element_type=jnp.float32)
         back_gate = (back * upper * sigma * (1.0 + gate * (1.0 - sigma))).astype(jnp.bfloat16)
         back_upper = (back * active).astype(jnp.bfloat16)
         moment_in[:, :hidden_units] += contract_rows(keyed, back_gate)
         moment_in[:, hidden_units:] += contract_rows(keyed, back_upper)
 
-    def renormalize(state, moment, base, copy, cols):
-        trial = state[:, cols] - moment[:, cols]
-        mean = jnp.mean(trial * trial, axis=0, keepdims=True)
-        state[:, cols] = trial * base[:, cols] * lax.rsqrt(mean + norm_eps)
-        copy[:, cols] = state[:, cols].astype(jnp.bfloat16)
-        moment[:, cols] = moment[:, cols] * momentum_keep
+    def renormalize(state, moment, base, axis):
+        trial = state - moment
+        mean = jnp.mean(trial * trial, axis=axis, keepdims=True)
+        return trial * base * lax.rsqrt(mean + norm_eps)
 
     for s in range(spans):
         for d in range(tok_count):
-            core_own[s][d].wait_recv()
-            core_far[s][d].wait_recv()
-        lax.fori_loop(0, tok_count, lambda t, c: (add_grads(s, t), c)[1], 0)
-        if s + 1 < spans:
-            for d in range(tok_count):
-                along_y[s + 1][d].wait_recv()
-                core_far[s + 1][d].start()
+            add_grads(s, d)
+            if s + 1 < spans:
+                if tok_count + 1 + d <= last_step:
+                    forward(s + 1, tok_count + 1 + d)
         for t in range(tok_count):
-            renormalize(state_in, moment_in, base_in, copy_in, slice(t * block_in, (t + 1) * block_in))
-        renormalize(state_out, moment_out, base_out, copy_out, slice(None))
-        made = fast_apply(queries[s], copy_in[...], copy_out[...])
+            cols = slice(t * block_in, (t + 1) * block_in)
+            fresh = renormalize(state_in[:, cols], moment_in[:, cols], base_in[:, cols], 0)
+            copy_in[:, cols] = fresh.astype(jnp.bfloat16)
+            if s + 1 < spans:
+                state_in[:, cols] = fresh
+                moment_in[:, cols] *= momentum_keep
+            turned = slice(t * block_out, (t + 1) * block_out)
+            fresh = renormalize(state_out[turned], moment_out[turned], base_out[turned], 1)
+            copy_out[turned] = fresh.astype(jnp.bfloat16)
+            if s + 1 < spans:
+                state_out[turned] = fresh
+                moment_out[turned] *= momentum_keep
+        pre_act = jnp.dot(queries[s], copy_in[...], preferred_element_type=jnp.float32)
+        gate = pre_act[:, :hidden_units]
+        hidden = (gate * jax.nn.sigmoid(gate) * pre_act[:, hidden_units:]).astype(jnp.bfloat16)
+        made = contract_cols(hidden, copy_out[...])
         produced[s] = made
         sums = jnp.sum(made * made, axis=1, keepdims=True)
         squares[s, head] = jnp.transpose(jnp.broadcast_to(sums, (rows, 128)))[:8]
@@ -400,7 +430,7 @@
     _, head_size, block_in = fast_in.shape
     _, hidden_units, block_out = fast_out.shape
     piece = width // (grp_count * head_count)
-    pack = block_out * (hidden_units // head_size)
+    fold = hidden_units * block_out // head_size
     dma = pltpu.SemaphoreType.DMA
     vmem = pltpu.VMEM
     pair = [dma((spans, tok_count))] * 2
@@ -411,16 +441,18 @@
         out_specs=pl.BlockSpec(memory_space=pltpu.VMEM),
         scratch_shapes=[
             vmem((spans, tok_count, head_count, grp_count, rows, piece), jnp.bfloat16),
-            vmem((tok_count, head_size, block_in + pack), jnp.bfloat16),
+            vmem((tok_count, head_size, block_in + fold), jnp.bfloat16),
             vmem((spans, rows, head_size), jnp.bfloat16),
+            vmem((spans, tok_count, rows, head_size), jnp.bfloat16),
+            vmem((spans, tok_count, rows, head_size), jnp.bfloat16),
             vmem((head_size, 2 * hidden_units), jnp.float32),
-            vmem((hidden_units, head_size), jnp.float32),
+            vmem((head_size, hidden_units), jnp.float32),
             vmem((head_size, 2 * hidden_units), jnp.float32),
-            vmem((hidden_units, head_size), jnp.float32),
+            vmem((head_size, hidden_units), jnp.float32),
             vmem((head_size, 2 * hidden_units), jnp.bfloat16),
-            vmem((hidden_units, head_size), jnp.bfloat16),
+            vmem((head_size, hidden_units), jnp.bfloat16),
             vmem((1, 2 * hidden_units), jnp.float32),
-            vmem((1, head_size), jnp.float32),
+            vmem((head_size, 1), jnp.float32),
             vmem((spans, rows, head_size), jnp.float32),
             vmem((spans, head_count, 8, rows), jnp.float32),
             dma((spans,)),
@@ -432,7 +464,10 @@
         ],
         compiler_params=pltpu.CompilerParams(collective_id=0, has_side_effects=True),
         name="fused_layer",
-    )(views, q_weight, k_weight, v_weight, rate_weight, fast_in, fast_out, out_gain.reshape(1, -1))
+    )(
+        views, q_weight, k_weight, v_weight, rate_weight.T, fast_in,
+        jnp.swapaxes(fast_out, 1, 2), out_gain.reshape(1, -1),
+    )
 
 
 def local(sizes, views, *rest):
@@ -443,8 +478,8 @@
     few = tok_count * views.shape[2] <= 4 * head_size
     fits = (
         tok_count > 1 and grp_count == 2 and head_count == 4 and piece % 128 == 0
-        and fast_in.shape[2] % 128 == 0 and views.shape[2] % 16 == 0 and hidden_units % head_size == 0
-        and fast_out.shape[2] * (hidden_units // head_size) % 128 == 0
+        and fast_in.shape[2] % 128 == 0 and views.shape[2] % 16 == 0 and head_size % fast_out.shape[2] == 0
+        and fast_out.shape[2] * hidden_units % (128 * head_size) == 0 and fast_out.shape[2] % 16 == 0
     )
     if few and fits:
         return by_kernel(sizes, views, *rest)

time: 56.8 us -> 52.7 us (0.928)
  local copies, waits for them, and re-layouts: 4.04 us -> 1.62 us
  Pallas kernels: 52.5 us -> 50.9 us
    unnamed x5 -> x1, local copies, waits for them, and re-layouts: 4.04 us -> 1.62 us
    pallas_call x1, Pallas kernels: 52.5 us -> 50.9 us  [by_kernel(): pl.pallas_call(functools.partial(fused_kernel, tok_count, grp_count, head...]
where the time goes in v2:
time: 52.7 us; the launch traced here: 52.6 us
  Pallas kernels  50.9 us (97%)
  local copies, waits for them, and re-layouts  1.62 us (3%)
    pallas_call x1, Pallas kernels, by_kernel(): pl.pallas_call(functools.partial(fused_kernel, tok_count, grp_count, head...  50.9 us
    unnamed x1, local copies, waits for them, and re-layouts  1.62 us

profile of v2, /device:TPU:0, one launch (start us, length us, event | category | flops | bytes accessed | tf_op | source)
XLA Modules:
  0.0 52.6 jit_solution(20930209665069033)
XLA Ops:
  0.0 50.9 %fused_layer.1 = bf16[1,2,192,256]{3,2,1,0:T(8,128)(2,1)} custom-call(bf16[1,2,192,1024]{3,2,1,0:T(8,128)(2,1)} %views_ref.1, bf16[1024,256]{1,0:T(8,128)(2,1)} %q_ref.1, bf16[1024,256]{1,0:T(8,128)(2,1)} %k_ref.1, bf16[1024,256]{1,0:T(8,128)(2,1)} %v_ref.1, bf16[1,1024]{1,0:T(2,128)(2,1)} %bitcast.4, f32[1,256,256]{2,1,0:T(8,128)} %in_ref.1, ...), custom_call_target="tpu_custom_call" | custom-call | tf_op jit(solution)/shard_map/fused_layer/pallas_call | solution.py:437
  50.9 1.6 %copy.10 = bf16[1,2,192,256]{3,2,1,0:T(8,128)(2,1)} copy(bf16[1,2,192,256]{3,2,1,0:T(8,128)(2,1)} %fused_layer.1) | data formatting | bytes 393216
